TPU v7x, 32 devices: a whole 2x2x4 slice. The times are simulated.
32 devices in a mesh: dp: 16 (over z, y, x), mp: 2 (over core).
Axes of the slice: x: 2, y: 2, z: 4, core: 2. Of those that a mesh axis runs over, the one named last changes fastest.
Arguments:
- gradient: bfloat16 [2, 8, 512, 512], P('mp', None, 'dp'), may hold values from -54 to 54
- owners: int32 [2, 8], P('mp'), may hold values from 0 to 15, as said below
- left_stats: float32 [2, 16, 512, 512], P('mp', 'dp'), may hold values from -0.2 to 20.2
- right_stats: float32 [2, 16, 512, 512], P('mp', 'dp'), may hold values from -0.2 to 20.2
- left_roots_old: bfloat16 [2, 16, 512, 512], P('mp', 'dp'), may hold values from -0.1 to 1.5
- right_roots_old: bfloat16 [2, 16, 512, 512], P('mp', 'dp'), may hold values from -0.1 to 1.5
Outputs:
- update: bfloat16 [2, 8, 512, 512], P('mp', None, 'dp')
- left_roots: bfloat16 [2, 16, 512, 512], P('mp', 'dp')
- right_roots: bfloat16 [2, 16, 512, 512], P('mp', 'dp')
Inputs may be any that keep to these rules, and one draw needn't show every extreme that they name: In each row the 8 owners are distinct. Owner o holds a block of row m exactly when owner (o + 8) mod 16 of row m holds none, and exactly when owner o of row (m + 1) mod 2 holds none.
All inputs are finite; a program needn't handle non-finite values.
Results may differ from a plain program's by a relative error of at most 0.0067.
Values may be sent and summed in bfloat16 or wider, within the bound.
A program may use at most 64 MiB of HBM per device.

v0:
```python
import jax
import jax.numpy as jnp
from jax import lax
from jax.sharding import PartitionSpec as P

ITERS = 2
stat_decay = 0.9
ridge_term = 0.001
tiny_term = 1e-06


def newton_root(statistic):
    dimension = statistic.shape[0]
    identity = jnp.eye(dimension, dtype=jnp.float32)
    shifted = statistic + ridge_term * identity
    norm_scale = jnp.sqrt(jnp.sum(shifted * shifted) + tiny_term)
    matrix = shifted / norm_scale
    iterate = identity
    for iteration in range(ITERS):
        factor = ((5.0 * identity - matrix) / 4.0).astype(jnp.bfloat16)
        if iteration == 0:
            iterate = norm_scale ** (-0.25) * lax.optimization_barrier(factor).astype(jnp.float32)
        else:
            iterate = jnp.dot(
                iterate.astype(jnp.bfloat16), factor, preferred_element_type=jnp.float32
            )
        if iteration + 1 < ITERS:
            factor_two = jnp.dot(factor, factor, preferred_element_type=jnp.float32).astype(
                jnp.bfloat16
            )
            factor_four = jnp.dot(
                factor_two, factor_two, preferred_element_type=jnp.float32
            ).astype(jnp.bfloat16)
            matrix = jnp.dot(
                factor_four, matrix.astype(jnp.bfloat16), preferred_element_type=jnp.float32
            )
    return iterate.astype(jnp.bfloat16)


def shards(gradient, owners, left_stats, right_stats, left_roots_old, right_roots_old):
    dp_count = lax.axis_size("dp")
    my_index = lax.axis_index("dp")
    blocks_here = gradient.shape[1]
    row_count = gradient.shape[2]
    block_width = gradient.shape[3]
    owner_table = owners[0]
    owner_ids = jnp.arange(dp_count, dtype=jnp.int32)
    selector = (owner_table[None, :] == owner_ids[:, None]).astype(jnp.bfloat16)
    flat_grad = gradient[0].reshape(blocks_here, row_count * block_width)
    outgoing = jnp.dot(selector, flat_grad, preferred_element_type=jnp.float32).astype(jnp.bfloat16)
    outgoing = outgoing.reshape(dp_count, row_count, block_width)
    arrived = lax.all_to_all(outgoing, "dp", split_axis=0, concat_axis=1, tiled=True)
    grad_block = arrived[0]
    is_mine = owner_table == my_index
    mine_weight = is_mine.astype(jnp.float32)
    is_busy = jnp.any(is_mine)
    left_gram = jnp.einsum("ik,jk->ij", grad_block, grad_block, preferred_element_type=jnp.float32)
    right_gram = jnp.einsum("ki,kj->ij", grad_block, grad_block, preferred_element_type=jnp.float32)
    left_new = stat_decay * left_stats[0, 0] + left_gram / block_width
    right_new = stat_decay * right_stats[0, 0] + right_gram / block_width
    shaded = jnp.dot(grad_block, right_roots_old[0, 0], preferred_element_type=jnp.float32).astype(
        jnp.bfloat16
    )
    direction = jnp.dot(left_roots_old[0, 0], shaded, preferred_element_type=jnp.float32).astype(
        jnp.bfloat16
    )
    squares = jnp.stack(
        [
            jnp.sum(jnp.square(grad_block.astype(jnp.float32))),
            jnp.sum(jnp.square(direction.astype(jnp.float32))),
        ]
    )
    graft_terms = squares[:, None] * mine_weight[None, :]
    returned = lax.all_to_all(direction[None], "dp", split_axis=1, concat_axis=0, tiled=True)
    totals = lax.psum(graft_terms, ("dp", "mp"))
    graft_scale = jnp.sqrt(totals[0] / (totals[1] + tiny_term))
    pieces = jnp.einsum(
        "on,or->nr",
        selector,
        returned.reshape(dp_count, row_count * block_width),
        preferred_element_type=jnp.float32,
    )
    update = (
        (graft_scale[:, None] * pieces)
        .astype(jnp.bfloat16)
        .reshape(1, blocks_here, row_count, block_width)
    )
    zero_root = jnp.zeros((block_width, block_width), jnp.bfloat16)
    left_root, right_root = lax.cond(
        is_busy,
        lambda: (newton_root(left_new), newton_root(right_new)),
        lambda: (zero_root, zero_root),
    )
    return (update, left_root[None, None], right_root[None, None])


def solution(mesh):
    return jax.shard_map(
        shards,
        mesh=mesh,
        in_specs=(
            P("mp", None, "dp", None),
            P("mp", None),
            P("mp", "dp", None, None),
            P("mp", "dp", None, None),
            P("mp", "dp", None, None),
            P("mp", "dp", None, None),
        ),
        out_specs=(P("mp", None, "dp", None), P("mp", "dp", None, None), P("mp", "dp", None, None)),
        check_vma=False,
    )
```

profile of v0, /device:TPU:0, one launch (start us, length us, event | category | flops | bytes accessed | tf_op | source)
XLA Modules:
  0.0 111.4 jit_solution(4444039082128814350)
XLA Ops:
  0.6 0.0 copy-start
  0.6 1.2 %copy.18 = bf16[1,8,32,512]{3,1,2,0:T(8,128)(2,1)S(1)} copy(bf16[1,8,32,512]{3,2,1,0:T(8,128)(2,1)} %param.8) | data formatting | bytes 524288
  1.8 0.0 copy-start.4
  1.8 0.6 copy-done.4
  2.5 0.3 convolution_convert_fusion.6
  2.7 1.0 copy.19
  3.7 0.0 copy-start.5
  3.7 8.5 %all-to-all-start = ((bf16[16,32,512]{2,1,0:T(8,128)(2,1)}), bf16[16,32,512]{2,1,0:T(8,128)(2,1)S(1)}, u32[]{:S(2)}, u32[]{:S(2)}) async-start(bf16[16,32,512]{2,1,0:T(8,128)(2,1)} %bitcast.21), calls=%async_computation | async-start | bytes 1048576 | tf_op jit(solution)/shard_map/all_to_all | solution.py:52
  12.2 0.6 compare_reduce_fusion
  12.8 14.4 %all-to-all-done = bf16[16,32,512]{2,1,0:T(8,128)(2,1)S(1)} async-done(((bf16[16,32,512]{2,1,0:T(8,128)(2,1)}), bf16[16,32,512]{2,1,0:T(8,128)(2,1)S(1)}, u32[]{:S(2)}, u32[]{:S(2)}) %all-to-all-start) | async-done | bytes 524320 | tf_op jit(solution)/shard_map/all_to_all | solution.py:52
  27.3 0.0 copy-done
  27.3 0.0 copy-done.5
  27.3 1.5 %multiply_reduce_fusion.2 = (f32[]{:T(128)}, bf16[512,512]{1,0:T(8,128)(2,1)S(1)}) fusion(bf16[1,1,512,512]{3,2,1,0:T(8,128)(2,1)S(1)} %copy-done, bf16[512,512]{1,0:T(8,128)(2,1)S(1)} %bitcast.76, bf16[1,1,512,512]{3,2,1,0:T(8,128)(2,1)S(1)} %copy-done.5), kind=kOutput, calls=%fused_computation.53 | convolution fusion | flops 538181632 | bytes 2097156 | tf_op jit(solution)/shard_map/dot_general | solution.py:64
  28.8 0.9 copy.16
  29.7 0.5 broadcast.160
  30.2 3.8 %reduce.3 = bf16[512,512]{1,0:T(8,128)(2,1)S(1)} reduce(bf16[512,1,512]{2,1,0:T(2,128)(2,1)S(1)} %bitcast.78, bf16[]{:T(256)} %broadcast.160), dimensions={1}, to_apply=%bitcast.56.reduce_sub_computation | reduce | bytes 1048578
  34.0 1.2 %reshape.49 = bf16[16,2,8192]{2,1,0:T(2,128)(2,1)} reshape(bf16[512,512]{1,0:T(8,128)(2,1)S(1)} %reduce.3) | data formatting | bytes 1048576
  35.2 4.2 %all-to-all-start.1 = ((bf16[16,2,8192]{2,1,0:T(2,128)(2,1)}), bf16[16,2,8192]{2,1,0:T(2,128)(2,1)}, u32[]{:S(2)}, u32[]{:S(2)}) async-start(bf16[16,2,8192]{2,1,0:T(2,128)(2,1)} %reshape.49), calls=%async_computation.1 | async-start | bytes 1048576 | tf_op jit(solution)/shard_map/all_to_all | solution.py:74
  39.5 0.9 multiply_reduce_fusion.3
  40.3 1.4 %pad_maximum_fusion = f32[2]{0:T(128)S(1)} fusion(f32[1]{0:T(128)} %bitcast.6, f32[1]{0:T(128)} %bitcast.1), kind=kLoop, calls=%fused_computation.63 | loop fusion | flops 2 | bytes 16 | tf_op jit(solution)/shard_map/stack | solution.py:67
  41.7 0.1 broadcast_multiply_fusion
  42.4 40.7 %psum.7 = f32[2,8]{1,0:T(2,128)S(1)} all-reduce(f32[2,8]{1,0:T(2,128)S(1)} %broadcast_multiply_fusion), channel_id=1, replica_groups=mesh['dp'=16,'mp'=2] {'dp','mp'}, use_global_device_ids=true, to_apply=%region_2.0 | all-reduce | flops 16 | bytes 128 | tf_op jit(solution)/shard_map/psum | solution.py:75
  83.1 0.5 fusion.37
  83.6 0.0 copy-start.1
  83.6 1.5 %convolution_bitcast_fusion = f32[512,512]{1,0:T(8,128)} fusion(bf16[16,32,512]{2,1,0:T(8,128)(2,1)S(1)} %all-to-all-done), kind=kOutput, calls=%fused_computation.50 | convolution fusion | flops 268435456 | bytes 1572864 | tf_op jit(solution)/shard_map/ki,kj->ij/dot_general | solution.py:58
  85.1 0.0 copy-done.1
  85.1 18.9 %conditional.1 = (bf16[1,1,512,512]{3,2,1,0:T(8,128)(2,1)S(1)}, bf16[1,1,512,512]{3,2,1,0:T(8,128)(2,1)}) conditional(s32[]{:T(128)} %convert_element_type.101, () %tuple.22, (f32[1,1,512,512]{3,2,1,0:T(8,128)S(1)}, f32[512,512]{1,0:T(8,128)S(1)}, f32[1,1,512,512]{3,2,1,0:T(8,128)}, f32[512,512]{1,0:T(8,128)}) %tuple.39), branch_computations={%region_4.0_spmd, %region_5.0_spmd.clone} | conditional | flops 2166620160 | bytes 20971660 | solution.py:89
  85.1 0.9 multiply_reduce_fusion.1
  86.7 2.4 %multiply_reduce_fusion = f32[]{:T(128)} fusion(f32[512,512]{1,0:T(8,128)} %get-tuple-element.58, f32[1,1,512,512]{3,2,1,0:T(8,128)} %get-tuple-element.60), kind=kLoop, calls=%fused_computation.25 | loop fusion | flops 2097151 | bytes 2097156 | tf_op jit(solution)/shard_map/cond/branch_1_fun/reduce_sum | solution.py:16
  89.8 2.9 %fusion.7 = (bf16[512,512]{1,0:T(8,128)(2,1)S(1)}, bf16[512,512]{1,0:T(8,128)(2,1)}) fusion(f32[]{:T(128)S(6)} %sqrt.20, f32[512,512]{1,0:T(8,128)S(1)} %get-tuple-element.57, f32[1,1,512,512]{3,2,1,0:T(8,128)S(1)} %get-tuple-element.59, f32[]{:T(128)S(6)} %sqrt.21, f32[512,512]{1,0:T(8,128)} %get-tuple-element.58, f32[1,1,512,512]{3,2,1,0:T(8,128)} %get-tuple-element.60), kind=kLoop, calls=%fused_computation.19 | loop fusion | flops 4980736 | bytes 5242888 | tf_op jit(solution)/shard_map/cond/branch_1_fun/convert_element_type | solution.py:20
  92.7 0.0 copy-start.3
  92.7 3.6 %convolution_convert_fusion.1 = bf16[512,512]{1,0:T(8,128)(2,1)} fusion(bf16[512,512]{1,0:T(8,128)(2,1)} %get-tuple-element.75), kind=kOutput, calls=%fused_computation.9 | convolution fusion | flops 537395200 | bytes 1048576 | tf_op jit(solution)/shard_map/cond/branch_1_fun/dot_general | solution.py:31
  96.4 3.5 %fusion.5 = bf16[1,1,512,512]{3,2,1,0:T(8,128)(2,1)} fusion(bf16[512,512]{1,0:T(8,128)(2,1)} %convolution_convert_fusion.1, bf16[512,512]{1,0:T(8,128)(2,1)} %get-tuple-element.75, f32[]{:T(128)S(6)} %pow.9, f32[]{:T(128)S(6)} %sqrt.21, f32[1,1,512,512]{3,2,1,0:T(8,128)} %get-tuple-element.60, f32[512,512]{1,0:T(8,128)} %get-tuple-element.58), kind=kOutput, calls=%fused_computation.17 | convolution fusion | flops 541327360 | bytes 3670024 | tf_op jit(solution)/shard_map/cond/branch_1_fun/dot_general | solution.py:24
  99.9 0.0 copy-done.3
  99.9 1.8 %convolution_convert_fusion.4 = bf16[512,512]{1,0:T(8,128)(2,1)} fusion(bf16[512,512]{1,0:T(8,128)(2,1)S(1)} %get-tuple-element.74), kind=kOutput, calls=%fused_computation.12 | convolution fusion | flops 537395200 | bytes 1048576 | tf_op jit(solution)/shard_map/cond/branch_1_fun/dot_general | solution.py:31
  101.8 2.1 %fusion.4 = bf16[1,1,512,512]{3,2,1,0:T(8,128)(2,1)S(1)} fusion(bf16[512,512]{1,0:T(8,128)(2,1)} %convolution_convert_fusion.4, bf16[512,512]{1,0:T(8,128)(2,1)} %copy-done.3, f32[]{:T(128)S(6)} %pow.8, f32[]{:T(128)S(6)} %sqrt.20, f32[1,1,512,512]{3,2,1,0:T(8,128)S(1)} %get-tuple-element.59, f32[512,512]{1,0:T(8,128)S(1)} %get-tuple-element.57), kind=kOutput, calls=%fused_computation.16 | convolution fusion | flops 541327360 | bytes 3670024 | tf_op jit(solution)/shard_map/cond/branch_1_fun/dot_general | solution.py:24
  104.0 0.0 copy-start.2
  104.0 0.8 copy-done.2
  104.8 0.0 all-to-all-done.1
  104.8 2.2 %reshape.50 = bf16[512,1,512]{2,1,0:T(2,128)(2,1)S(1)} reshape(bf16[16,2,8192]{2,1,0:T(2,128)(2,1)} %all-to-all-done.1) | data formatting | bytes 1048576
  107.0 3.1 %bitcast_reduce_fusion = bf16[512,512]{1,0:T(8,128)(2,1)S(1)} fusion(bf16[512,1,512]{2,1,0:T(2,128)(2,1)S(1)} %reshape.50), kind=kLoop, calls=%fused_computation.67 | loop fusion | bytes 1048576 | tf_op jit(solution)/shard_map/all_to_all | solution.py:74
  110.1 0.2 reshape.40
  110.4 0.3 fusion.28
  110.7 0.8 copy.17
  (2 shorter events, 0.0 us)
Async XLA Ops:
  0.6 26.6 %copy-start = (bf16[1,1,512,512]{3,2,1,0:T(8,128)(2,1)S(1)}, bf16[1,1,512,512]{3,2,1,0:T(8,128)(2,1)}, u32[]{:S(2)}) copy-start(bf16[1,1,512,512]{3,2,1,0:T(8,128)(2,1)} %param.12) | copy-start | bytes 1572868
  1.8 0.7 copy-start.4
  3.7 23.6 %copy-start.5 = (bf16[1,1,512,512]{3,2,1,0:T(8,128)(2,1)S(1)}, bf16[1,1,512,512]{3,2,1,0:T(8,128)(2,1)}, u32[]{:S(2)}) copy-start(bf16[1,1,512,512]{3,2,1,0:T(8,128)(2,1)} %param.13) | copy-start | bytes 1572868
  3.7 23.6 %all-to-all-start = ((bf16[16,32,512]{2,1,0:T(8,128)(2,1)}), bf16[16,32,512]{2,1,0:T(8,128)(2,1)S(1)}, u32[]{:S(2)}, u32[]{:S(2)}) async-start(bf16[16,32,512]{2,1,0:T(8,128)(2,1)} %bitcast.21), calls=%async_computation | async-start | bytes 1048576 | tf_op jit(solution)/shard_map/all_to_all | solution.py:52
  35.2 69.6 %all-to-all-start.1 = ((bf16[16,2,8192]{2,1,0:T(2,128)(2,1)}), bf16[16,2,8192]{2,1,0:T(2,128)(2,1)}, u32[]{:S(2)}, u32[]{:S(2)}) async-start(bf16[16,2,8192]{2,1,0:T(2,128)(2,1)} %reshape.49), calls=%async_computation.1 | async-start | bytes 1048576 | tf_op jit(solution)/shard_map/all_to_all | solution.py:74
  83.6 1.5 %copy-start.1 = (f32[1,1,512,512]{3,2,1,0:T(8,128)S(1)}, f32[1,1,512,512]{3,2,1,0:T(8,128)}, u32[]{:S(2)}) copy-start(f32[1,1,512,512]{3,2,1,0:T(8,128)} %param.10) | copy-start | bytes 3145732
  92.7 7.2 %copy-start.3 = (bf16[512,512]{1,0:T(8,128)(2,1)}, bf16[512,512]{1,0:T(8,128)(2,1)S(1)}, u32[]{:S(2)}) copy-start(bf16[512,512]{1,0:T(8,128)(2,1)S(1)} %get-tuple-element.74) | copy-start | bytes 1572868 | tf_op jit(solution)/shard_map/cond
  104.0 0.8 copy-start.2
where the time goes:
time: 112 us; the launch traced here: 111 us
  blocking collectives  40.7 us (36%)
  matrix products  15 us (13%)
  waiting for transfers between devices  14.4 us (13%)
  other arithmetic  13 us (12%)
  starting transfers between devices  12.7 us (11%)
  local copies, waits for them, and re-layouts  12.5 us (11%)
  loops' own time  1.68 us (2%)
  between operations  1.41 us (1%)
    psum x1, blocking collectives, shards(): totals = lax.psum(graft_terms, ('dp', 'mp'))  40.7 us
    all_to_all x1, waiting for transfers between devices, shards(): lax.all_to_all(outgoing, 'dp', split_axis=0, concat_axis=1, tiled=True)  14.4 us
    all_to_all x1, starting transfers between devices, shards(): lax.all_to_all(outgoing, 'dp', split_axis=0, concat_axis=1, tiled=True)  8.47 us
    unnamed x16, local copies, waits for them, and re-layouts  8.25 us
    dot_general x2, matrix products, newton_root(): jnp.dot(iterate.astype(jnp.bfloat16), factor, preferred_element_type=jnp....  5.58 us
    dot_general x2, matrix products, newton_root(): jnp.dot(factor_two, factor_two, preferred_element_type=jnp.float32)  5.42 us
    all_to_all x1, starting transfers between devices, shards(): lax.all_to_all(direction[None], 'dp', split_axis=1, concat_axis=0, tiled=...  4.23 us
    unnamed x1, other arithmetic  3.82 us
  transfers between devices with their start and end apart: 2, of which 1 were waited for; matrix products, arithmetic and copies ran while one was open for 20% of the time, Pallas kernels for 0%

commit v1 on v0

--- a/solution.py
+++ b/solution.py
@@ -72,7 +72,7 @@
     )
     graft_terms = squares[:, None] * mine_weight[None, :]
     returned = lax.all_to_all(direction[None], "dp", split_axis=1, concat_axis=0, tiled=True)
-    totals = lax.psum(graft_terms, ("dp", "mp"))
+    totals = jax.lax.psum(jax.lax.psum(graft_terms, "mp"), "dp")
     graft_scale = jnp.sqrt(totals[0] / (totals[1] + tiny_term))
     pieces = jnp.einsum(
         "on,or->nr",

time: 112 us -> 118 us (1.054)
  blocking collectives: 40.7 us -> 44.6 us
  matrix products: 15 us -> 17.6 us
    psum x1 -> x2, blocking collectives: 40.7 us -> 44.6 us  [shards(): totals = jax.lax.psum(jax.lax.psum(graft_terms, 'mp'), 'dp')]
    dot_general x2, matrix products: 5.42 us -> 7.18 us  [newton_root(): jnp.dot(factor_two, factor_two, preferred_element_type=jnp.float32)]
    unnamed x16 -> x14, local copies, waits for them, and re-layouts: 8.25 us -> 8.24 us
  transfers between devices with their start and end apart: 2 -> 2, of which waited for: 1 -> 1; matrix products, arithmetic and copies ran while one was open for 20% -> 21% of each run, Pallas kernels for 0% -> 0%
where the time goes in v1:
time: 118 us; the launch traced here: 117 us
  blocking collectives  44.6 us (38%)
  matrix products  17.6 us (15%)
  waiting for transfers between devices  13.8 us (12%)
  other arithmetic  13.3 us (11%)
  starting transfers between devices  12.7 us (11%)
  local copies, waits for them, and re-layouts  12.4 us (11%)
  loops' own time  1.5 us (1%)
  between operations  1.39 us (1%)
    psum x2, blocking collectives, shards(): totals = jax.lax.psum(jax.lax.psum(graft_terms, 'mp'), 'dp')  44.6 us
    all_to_all x1, waiting for transfers between devices, shards(): lax.all_to_all(outgoing, 'dp', split_axis=0, concat_axis=1, tiled=True)  13.8 us
    all_to_all x1, starting transfers between devices, shards(): lax.all_to_all(outgoing, 'dp', split_axis=0, concat_axis=1, tiled=True)  8.47 us
    unnamed x14, local copies, waits for them, and re-layouts  8.24 us
    dot_general x2, matrix products, newton_root(): jnp.dot(factor_two, factor_two, preferred_element_type=jnp.float32)  7.18 us
    dot_general x2, matrix products, newton_root(): jnp.dot(iterate.astype(jnp.bfloat16), factor, preferred_element_type=jnp....  6.38 us
    all_to_all x1, starting transfers between devices, shards(): lax.all_to_all(direction[None], 'dp', split_axis=1, concat_axis=0, tiled=...  4.23 us
    unnamed x1, other arithmetic  3.82 us
  transfers between devices with their start and end apart: 2, of which 1 were waited for; matrix products, arithmetic and copies ran while one was open for 21% of the time, Pallas kernels for 0%

profile of v1, /device:TPU:0, one launch (start us, length us, event | category | flops | bytes accessed | tf_op | source)
XLA Modules:
  0.0 117.3 jit_solution(14797833556148512014)
XLA Ops:
  0.6 0.0 copy-start
  0.6 1.2 copy.18
  1.8 0.0 copy-start.2
  1.8 0.6 copy-done.2
  2.5 0.3 convolution_convert_fusion.6
  2.7 1.0 copy.19
  3.7 0.0 copy-start.3
  3.7 8.5 %all-to-all-start = ((bf16[16,32,512]{2,1,0:T(8,128)(2,1)}), bf16[16,32,512]{2,1,0:T(8,128)(2,1)S(1)}, u32[]{:S(2)}, u32[]{:S(2)}) async-start(bf16[16,32,512]{2,1,0:T(8,128)(2,1)} %bitcast.21), calls=%async_computation | async-start | bytes 1048576 | tf_op jit(solution)/shard_map/all_to_all | solution.py:52
  12.2 0.6 compare_reduce_fusion
  13.5 13.8 %all-to-all-done = bf16[16,32,512]{2,1,0:T(8,128)(2,1)S(1)} async-done(((bf16[16,32,512]{2,1,0:T(8,128)(2,1)}), bf16[16,32,512]{2,1,0:T(8,128)(2,1)S(1)}, u32[]{:S(2)}, u32[]{:S(2)}) %all-to-all-start) | async-done | bytes 524320 | tf_op jit(solution)/shard_map/all_to_all | solution.py:52
  27.3 0.0 copy-done
  27.3 0.0 copy-done.3
  27.3 1.5 %multiply_reduce_fusion.2 = (f32[]{:T(128)}, bf16[512,512]{1,0:T(8,128)(2,1)S(1)}) fusion(bf16[1,1,512,512]{3,2,1,0:T(8,128)(2,1)S(1)} %copy-done, bf16[512,512]{1,0:T(8,128)(2,1)S(1)} %bitcast.76, bf16[1,1,512,512]{3,2,1,0:T(8,128)(2,1)S(1)} %copy-done.3), kind=kOutput, calls=%fused_computation.53 | convolution fusion | flops 538181632 | bytes 2097156 | tf_op jit(solution)/shard_map/dot_general | solution.py:64
  28.8 0.9 copy.16
  29.7 0.5 broadcast.160
  30.2 3.8 %reduce.3 = bf16[512,512]{1,0:T(8,128)(2,1)S(1)} reduce(bf16[512,1,512]{2,1,0:T(2,128)(2,1)S(1)} %bitcast.78, bf16[]{:T(256)} %broadcast.160), dimensions={1}, to_apply=%bitcast.56.reduce_sub_computation | reduce | bytes 1048578
  34.0 1.2 %reshape.49 = bf16[16,2,8192]{2,1,0:T(2,128)(2,1)} reshape(bf16[512,512]{1,0:T(8,128)(2,1)S(1)} %reduce.3) | data formatting | bytes 1048576
  35.2 4.2 %all-to-all-start.1 = ((bf16[16,2,8192]{2,1,0:T(2,128)(2,1)}), bf16[16,2,8192]{2,1,0:T(2,128)(2,1)}, u32[]{:S(2)}, u32[]{:S(2)}) async-start(bf16[16,2,8192]{2,1,0:T(2,128)(2,1)} %reshape.49), calls=%async_computation.1 | async-start | bytes 1048576 | tf_op jit(solution)/shard_map/all_to_all | solution.py:74
  39.5 1.5 %convolution_bitcast_fusion = f32[512,512]{1,0:T(8,128)} fusion(bf16[16,32,512]{2,1,0:T(8,128)(2,1)S(1)} %all-to-all-done), kind=kOutput, calls=%fused_computation.50 | convolution fusion | flops 268435456 | bytes 1572864 | tf_op jit(solution)/shard_map/ki,kj->ij/dot_general | solution.py:58
  40.9 0.0 copy-start.1
  40.9 0.5 fusion.37
  41.4 0.8 copy-done.1
  42.1 21.5 %conditional.1 = (bf16[1,1,512,512]{3,2,1,0:T(8,128)(2,1)}, bf16[1,1,512,512]{3,2,1,0:T(8,128)(2,1)}) conditional(s32[]{:T(128)} %convert_element_type.101, () %tuple.22, (f32[1,1,512,512]{3,2,1,0:T(8,128)S(1)}, f32[512,512]{1,0:T(8,128)S(1)}, f32[1,1,512,512]{3,2,1,0:T(8,128)}, f32[512,512]{1,0:T(8,128)}) %tuple.39), branch_computations={%region_5.0_spmd, %region_6.0_spmd.clone} | conditional | flops 2166620160 | bytes 18874480 | solution.py:89
  42.1 0.9 multiply_reduce_fusion.1
  43.8 2.4 %multiply_reduce_fusion = f32[]{:T(128)} fusion(f32[512,512]{1,0:T(8,128)} %get-tuple-element.58, f32[1,1,512,512]{3,2,1,0:T(8,128)} %get-tuple-element.60), kind=kLoop, calls=%fused_computation.25 | loop fusion | flops 2097151 | bytes 2097156 | tf_op jit(solution)/shard_map/cond/branch_1_fun/reduce_sum | solution.py:16
  46.9 3.1 %fusion.7 = (bf16[512,512]{1,0:T(8,128)(2,1)}, bf16[512,512]{1,0:T(8,128)(2,1)}) fusion(f32[]{:T(128)S(6)} %sqrt.20, f32[512,512]{1,0:T(8,128)S(1)} %get-tuple-element.57, f32[1,1,512,512]{3,2,1,0:T(8,128)S(1)} %get-tuple-element.59, f32[]{:T(128)S(6)} %sqrt.21, f32[512,512]{1,0:T(8,128)} %get-tuple-element.58, f32[1,1,512,512]{3,2,1,0:T(8,128)} %get-tuple-element.60), kind=kLoop, calls=%fused_computation.19 | loop fusion | flops 4980736 | bytes 5242888 | tf_op jit(solution)/shard_map/cond/branch_1_fun/convert_element_type | solution.py:20
  50.0 3.7 %convolution_convert_fusion.1 = bf16[512,512]{1,0:T(8,128)(2,1)} fusion(bf16[512,512]{1,0:T(8,128)(2,1)} %get-tuple-element.75), kind=kOutput, calls=%fused_computation.9 | convolution fusion | flops 537395200 | bytes 1048576 | tf_op jit(solution)/shard_map/cond/branch_1_fun/dot_general | solution.py:31
  53.7 3.5 %fusion.5 = bf16[1,1,512,512]{3,2,1,0:T(8,128)(2,1)} fusion(bf16[512,512]{1,0:T(8,128)(2,1)} %convolution_convert_fusion.1, bf16[512,512]{1,0:T(8,128)(2,1)} %get-tuple-element.75, f32[]{:T(128)S(6)} %pow.9, f32[]{:T(128)S(6)} %sqrt.21, f32[1,1,512,512]{3,2,1,0:T(8,128)} %get-tuple-element.60, f32[512,512]{1,0:T(8,128)} %get-tuple-element.58), kind=kOutput, calls=%fused_computation.17 | convolution fusion | flops 541327360 | bytes 3670024 | tf_op jit(solution)/shard_map/cond/branch_1_fun/dot_general | solution.py:24
  57.2 3.5 %convolution_convert_fusion.4 = bf16[512,512]{1,0:T(8,128)(2,1)} fusion(bf16[512,512]{1,0:T(8,128)(2,1)} %get-tuple-element.74), kind=kOutput, calls=%fused_computation.12 | convolution fusion | flops 537395200 | bytes 1048576 | tf_op jit(solution)/shard_map/cond/branch_1_fun/dot_general | solution.py:31
  60.8 2.9 %fusion.4 = bf16[1,1,512,512]{3,2,1,0:T(8,128)(2,1)} fusion(bf16[512,512]{1,0:T(8,128)(2,1)} %convolution_convert_fusion.4, bf16[512,512]{1,0:T(8,128)(2,1)} %get-tuple-element.74, f32[]{:T(128)S(6)} %pow.8, f32[]{:T(128)S(6)} %sqrt.20, f32[1,1,512,512]{3,2,1,0:T(8,128)S(1)} %get-tuple-element.59, f32[512,512]{1,0:T(8,128)S(1)} %get-tuple-element.57), kind=kOutput, calls=%fused_computation.16 | convolution fusion | flops 541327360 | bytes 3670024 | tf_op jit(solution)/shard_map/cond/branch_1_fun/dot_general | solution.py:24
  63.6 0.9 multiply_reduce_fusion.3
  64.6 1.4 %pad_maximum_fusion = f32[2]{0:T(128)S(1)} fusion(f32[1]{0:T(128)} %bitcast.6, f32[1]{0:T(128)} %bitcast.1), kind=kLoop, calls=%fused_computation.63 | loop fusion | flops 2 | bytes 16 | tf_op jit(solution)/shard_map/stack | solution.py:67
  66.0 0.1 broadcast_multiply_fusion
  66.1 2.4 %psum.14 = f32[2,8]{1,0:T(2,128)S(1)} all-reduce(f32[2,8]{1,0:T(2,128)S(1)} %broadcast_multiply_fusion), channel_id=1, replica_groups=mesh['dp'=16,'mp'=2] {'mp'}, use_global_device_ids=true, to_apply=%region_2.0 | all-reduce | flops 16 | bytes 128 | tf_op jit(solution)/shard_map/psum | solution.py:75
  68.5 42.1 %psum.15 = f32[2,8]{1,0:T(2,128)S(1)} all-reduce(f32[2,8]{1,0:T(2,128)S(1)} %psum.14), channel_id=1, replica_groups=mesh['dp'=16,'mp'=2] {'dp'}, use_global_device_ids=true, to_apply=%region_3.0 | all-reduce | flops 16 | bytes 128 | tf_op jit(solution)/shard_map/psum | solution.py:75
  110.7 0.0 all-to-all-done.1
  110.7 2.2 %reshape.50 = bf16[512,1,512]{2,1,0:T(2,128)(2,1)S(1)} reshape(bf16[16,2,8192]{2,1,0:T(2,128)(2,1)} %all-to-all-done.1) | data formatting | bytes 1048576
  112.9 3.1 %bitcast_reduce_fusion = bf16[512,512]{1,0:T(8,128)(2,1)S(1)} fusion(bf16[512,1,512]{2,1,0:T(2,128)(2,1)S(1)} %reshape.50), kind=kLoop, calls=%fused_computation.67 | loop fusion | bytes 1048576 | tf_op jit(solution)/shard_map/all_to_all | solution.py:74
  116.0 0.2 reshape.40
  116.2 0.3 fusion.28
  116.5 0.8 copy.17
  (2 shorter events, 0.0 us)
Async XLA Ops:
  0.6 26.6 %copy-start = (bf16[1,1,512,512]{3,2,1,0:T(8,128)(2,1)S(1)}, bf16[1,1,512,512]{3,2,1,0:T(8,128)(2,1)}, u32[]{:S(2)}) copy-start(bf16[1,1,512,512]{3,2,1,0:T(8,128)(2,1)} %param.12) | copy-start | bytes 1572868
  1.8 0.7 copy-start.2
  3.7 23.6 %copy-start.3 = (bf16[1,1,512,512]{3,2,1,0:T(8,128)(2,1)S(1)}, bf16[1,1,512,512]{3,2,1,0:T(8,128)(2,1)}, u32[]{:S(2)}) copy-start(bf16[1,1,512,512]{3,2,1,0:T(8,128)(2,1)} %param.13) | copy-start | bytes 1572868
  3.7 23.6 %all-to-all-start = ((bf16[16,32,512]{2,1,0:T(8,128)(2,1)}), bf16[16,32,512]{2,1,0:T(8,128)(2,1)S(1)}, u32[]{:S(2)}, u32[]{:S(2)}) async-start(bf16[16,32,512]{2,1,0:T(8,128)(2,1)} %bitcast.21), calls=%async_computation | async-start | bytes 1048576 | tf_op jit(solution)/shard_map/all_to_all | solution.py:52
  35.2 75.5 %all-to-all-start.1 = ((bf16[16,2,8192]{2,1,0:T(2,128)(2,1)}), bf16[16,2,8192]{2,1,0:T(2,128)(2,1)}, u32[]{:S(2)}, u32[]{:S(2)}) async-start(bf16[16,2,8192]{2,1,0:T(2,128)(2,1)} %reshape.49), calls=%async_computation.1 | async-start | bytes 1048576 | tf_op jit(solution)/shard_map/all_to_all | solution.py:74
  40.9 1.2 %copy-start.1 = (f32[1,1,512,512]{3,2,1,0:T(8,128)S(1)}, f32[1,1,512,512]{3,2,1,0:T(8,128)}, u32[]{:S(2)}) copy-start(f32[1,1,512,512]{3,2,1,0:T(8,128)} %param.10) | copy-start | bytes 3145732
